TPU v7x, 32 devices: a whole 2x2x4 slice. The times are simulated.
32 devices in a mesh: groups: 2 (over y), row: 4 (over z), col: 4 (over x, core).
Axes of the slice: x: 2, y: 2, z: 4, core: 2. Of those that a mesh axis runs over, the one named last changes fastest.
Arguments:
- slip: float32 [32, 16, 243], P(('groups', 'row', 'col')), parts along dimension 0, may hold values from -6 to 6
- inverse: float32 [32, 486, 243], P(('groups', 'row', 'col')), parts along dimension 0, may hold values from -0.6 to 0.6
- positions: float32 [32, 3, 81], P('groups'), parts along dimension 0
Outputs:
- updated: float32 [32, 16, 243], P(('groups', 'row', 'col')), parts along dimension 0
- residual: float32 [32, 16, 243], P(('groups', 'row', 'col')), parts along dimension 0
There are 2 independent parts, one for each index of `groups`. A program takes and returns all parts, laid end to end along the dimension named above; each array names one. Nothing has to cross between parts.
All inputs are finite; a program needn't handle non-finite values.
Results may differ from a plain program's by a relative error of at most 0.0041.
Values may be sent and summed in bfloat16 or wider, within the bound.
A program may use at most 64 MiB of HBM per device.

v0:
```python
import functools
import math

import jax
import jax.numpy as jnp
from jax import lax
from jax.experimental import pallas as pl
from jax.experimental.pallas import tpu as pltpu
from jax.sharding import PartitionSpec as P

MESH = pl.DeviceIdType.MESH
LANES = 128
CHUNK = 16
GROUP = 2


def round_up(value, step):
    return -(-value // step) * step


def split(value):
    high = value.astype(jnp.bfloat16)
    low = (value - high.astype(jnp.float32)).astype(jnp.bfloat16)
    return high, low


def triple(rows, blobs):
    lane = lax.broadcasted_iota(jnp.int32, rows.shape, rows.ndim - 1)
    axis = rows.ndim - 1
    once = pltpu.roll(rows, blobs, axis)
    twice = pltpu.roll(rows, 2 * blobs, axis)
    return jnp.where(lane < blobs, rows, jnp.where(lane < 2 * blobs, once, twice))


def kernel(
    row_count, col_count, blobs,
    slip_hbm, inverse_hbm, positions_hbm,
    updated, residual,
    slip, inverse, positions,
    inv_high, inv_low, tiles, own_rows, own, source, other_slip, part, other_part, forces, held,
    load_sems, slip_sems, part_sems, send_sems, recv_sems, go_sem,
):
    bodies = row_count * col_count // 2
    row = lax.axis_index("row")
    col = lax.axis_index("col")
    half = lax.rem(col, 2)
    partner = col + 1 - 2 * half
    body = (row * col_count + col) // 2
    narrow = 3 * blobs
    wide = source.shape[-1]
    pad = own.shape[2]

    barrier = pltpu.get_barrier_semaphore()

    low_side = row < row_count // 2

    def far(step):
        return jnp.where(low_side, bodies - 1 - step, step)

    def place(j):
        there = 2 * j + half
        return {"row": there // col_count, "col": lax.rem(there, col_count)}

    def each(action):
        def visit(step, carry):
            j = far(step)

            @pl.when(j != body)
            def _():
                action(j)

            return carry

        lax.fori_loop(0, bodies, visit, 0)

    def welcome(j):
        there = 2 * j
        device = {"row": there // col_count, "col": lax.rem(there, col_count)}
        pl.semaphore_signal(barrier, inc=1, device_id=device, device_id_type=MESH)

    each(welcome)

    @pl.when(half == 0)
    def _():
        pl.semaphore_signal(barrier, inc=1, device_id={"col": partner}, device_id_type=MESH)


    loads = [
        pltpu.make_async_copy(positions_hbm, positions, load_sems.at[0]),
        pltpu.make_async_copy(slip_hbm.at[0], slip, load_sems.at[1]),
        pltpu.make_async_copy(inverse_hbm.at[:, 0, :], inverse, load_sems.at[2]),
    ]
    for load in loads:
        load.start()
    inv_high[...] = jnp.zeros_like(inv_high)
    inv_low[...] = jnp.zeros_like(inv_low)
    own_rows[...] = jnp.zeros_like(own_rows)

    def build(step, carry):
        j = step // 2
        t = lax.rem(step, 2)
        lane = lax.broadcasted_iota(jnp.int32, (CHUNK, wide), 1)
        masks = [(lane >= a * blobs) & (lane < (a + 1) * blobs) for a in range(3)]
        there = [
            jnp.broadcast_to(source[a, pl.ds(2 * j + half, 1), :], (CHUNK, wide)) for a in range(4)
        ]
        for at in range(0, pad, CHUNK):
            d0, d1, d2, db = [own[t, a, at : at + CHUNK, :] - there[a] for a in range(4)]
            dist_sq = d0 * d0 + d1 * d1 + d2 * d2
            r = lax.rsqrt(jnp.where(dist_sq > 0.0, dist_sq, 1.0))
            r2 = r * r
            k = 0.75 * r
            u = k * r2
            far = dist_sq >= 4.0
            isotropic = jnp.where(far, k + (2.0 / 3.0) * u, 1.0 - (9.0 / 32.0) * (dist_sq * r))
            anisotropic = jnp.where(far, u - (2.0 * u) * r2, (3.0 / 32.0) * r)
            scaled = anisotropic * db
            for a, da in enumerate((d0, d1, d2)):
                value = scaled * da + jnp.where(masks[a], isotropic, 0.0)
                tiles[j, t, a * pad + at : a * pad + at + CHUNK, :] = value.astype(jnp.bfloat16)
        return carry

    loads[1].wait()

    def swap(source_ref, target_ref, sems):
        return pltpu.make_async_remote_copy(
            src_ref=source_ref,
            dst_ref=target_ref,
            send_sem=sems.at[0],
            recv_sem=sems.at[1],
            device_id={"col": partner},
            device_id_type=MESH,
        )

    slip_swap = swap(slip, other_slip, slip_sems)

    @pl.when(half == 1)
    def _():
        pl.semaphore_wait(barrier, 1)
        slip_swap.start()

    @pl.when(half == 0)
    def _():
        slip_swap.wait_recv()
        slip_swap.start()

    loads[2].wait()
    for h in range(2):
        high, low = split(inverse[h * narrow : (h + 1) * narrow, :])
        inv_high[h, :narrow, :narrow] = high
        inv_low[h, :narrow, :narrow] = low

    def apply(values, h):
        high, low = split(jnp.pad(values, ((0, 0), (0, wide - narrow))))
        big = inv_high[h]
        small = inv_low[h]
        rows = values.shape[0]
        both = jnp.dot(
            jnp.concatenate([high, low], axis=0), big, preferred_element_type=jnp.float32
        )
        cross = jnp.dot(high, small, preferred_element_type=jnp.float32)
        return both[:rows] + (both[rows:] + cross)

    force = apply(slip[...], half)
    slip_swap.wait_send()

    @pl.when(half == 1)
    def _():
        slip_swap.wait_recv()

    force = force + apply(other_slip[...], 1 - half)
    forces[body] = force.astype(jnp.bfloat16)
    held[...] = force

    def send(j):
        return pltpu.make_async_remote_copy(
            src_ref=forces.at[body],
            dst_ref=forces.at[body],
            send_sem=send_sems.at[j],
            recv_sem=recv_sems.at[body],
            device_id=place(j),
            device_id_type=MESH,
        )

    @pl.when(half == 0)
    def _():
        pl.semaphore_wait(barrier, 2 * (bodies - 1))
        pl.semaphore_signal(go_sem, inc=1, device_id={"col": partner}, device_id_type=MESH)

    @pl.when(half == 1)
    def _():
        pl.semaphore_wait(go_sem, 1)

    each(lambda j: send(j).start())

    loads[0].wait()

    lane = lax.broadcasted_iota(jnp.int32, source.shape[1:], 1)
    spread = []
    for a in range(3):
        rows = jnp.pad(positions[a], ((0, 0), (0, wide - blobs)))
        spread.append(triple(rows, blobs))
        source[a] = spread[a]
        for t in range(2):
            own_rows[3 * t + a : 3 * t + a + 1, :blobs] = positions[a, pl.ds(2 * body + t, 1), :]
    source[3] = jnp.where(
        lane < blobs, spread[0], jnp.where(lane < 2 * blobs, spread[1], spread[2])
    )
    own_cols = own_rows[...].T
    lane = lax.broadcasted_iota(jnp.int32, (pad, wide), 1)
    for t in range(2):
        cols = [
            jnp.broadcast_to(own_cols[:pad, 3 * t + a : 3 * t + a + 1], (pad, wide))
            for a in range(3)
        ]
        for a in range(3):
            own[t, a] = cols[a]
        own[t, 3] = jnp.where(lane < blobs, cols[0], jnp.where(lane < 2 * blobs, cols[1], cols[2]))

    lax.fori_loop(0, 2 * bodies, build, 0)

    def product(j):
        return lax.dot_general(
            forces[j],
            tiles[j].reshape(6 * pad, wide),
            (((1,), (1,)), ((), ())),
            preferred_element_type=jnp.float32,
        )

    def receive(j):
        @pl.when(j != body)
        def _():
            pltpu.make_async_remote_copy(
                src_ref=forces.at[j],
                dst_ref=forces.at[j],
                send_sem=send_sems.at[0],
                recv_sem=recv_sems.at[j],
                device_id={"col": partner},
                device_id_type=MESH,
            ).wait_recv()

    group = math.gcd(bodies, GROUP)

    def gather(turn, total):
        picks = [far(bodies - 1 - (turn * group + k)) for k in range(group)]
        for j in picks:
            receive(j)
        for j in picks:
            total = total + product(j)
        return total

    total = jnp.zeros((slip.shape[0], 6 * pad), jnp.float32)
    if bodies <= 8:
        for turn in range(bodies // group):
            total = gather(turn, total)
    else:
        total = lax.fori_loop(0, bodies // group, gather, total)
    full = round_up(6 * pad, LANES)
    total = jnp.pad(total, ((0, 0), (0, full - 6 * pad)))
    lane = lax.broadcasted_iota(jnp.int32, total.shape, 1)

    def moved(by):
        return pltpu.roll(total, full - by, 1) if by else total

    for t in range(2):
        start = 3 * t * pad
        shift = pad - blobs
        value = jnp.where(
            lane < blobs,
            moved(start),
            jnp.where(lane < 2 * blobs, moved(start + shift), moved(start + 2 * shift)),
        )
        part[t] = value[:, :wide]
    part_swap = swap(part, other_part, part_sems)
    part_swap.start()

    each(lambda j: send(j).wait_send())
    part_swap.wait()
    mine = slip[...] - (part[half] + other_part[half])[:, :narrow]
    residual[0] = mine
    theirs = other_slip[...] - (part[1 - half] + other_part[1 - half])[:, :narrow]
    result = held[...] + (apply(mine, half) + apply(theirs, 1 - half))
    updated[0] = result[:, :narrow]


def finish(updated, residual, updated_out, residual_out, sems):
    copies = [
        pltpu.make_async_copy(updated, updated_out, sems.at[0]),
        pltpu.make_async_copy(residual, residual_out, sems.at[1]),
    ]
    for copy in copies:
        copy.start()
    for copy in copies:
        copy.wait()


def stay(value):
    return pltpu.with_memory_space_constraint(value, pltpu.HBM)


def local(slip, inverse, positions):
    row_count = lax.axis_size("row")
    col_count = lax.axis_size("col")
    count = row_count * col_count
    bodies = count // 2
    blobs = positions.shape[2]
    rows, narrow = slip.shape[1:]
    wide = round_up(narrow, LANES)
    pad = round_up(blobs, CHUNK)
    vmem = pl.BlockSpec(memory_space=pltpu.VMEM)
    f32, bf16 = jnp.float32, jnp.bfloat16
    dma = pltpu.SemaphoreType.DMA
    tile_bytes = bodies * 6 * pad * wide * 2
    updated, residual = pl.pallas_call(
        functools.partial(kernel, row_count, col_count, blobs),
        out_shape=(
            pltpu.VMEM(slip.shape, f32),
            pltpu.VMEM(slip.shape, f32),
        ),
        in_specs=[pl.BlockSpec(memory_space=pltpu.HBM)] * 3,
        out_specs=(vmem, vmem),
        scratch_shapes=[
            pltpu.VMEM((rows, narrow), f32),
            pltpu.VMEM(inverse.shape[1:], f32),
            pltpu.VMEM((3, count, blobs), f32),
            pltpu.VMEM((2, wide, wide), bf16),
            pltpu.VMEM((2, wide, wide), bf16),
            pltpu.VMEM((bodies, 2, 3 * pad, wide), bf16),
            pltpu.VMEM((8, LANES), f32),
            pltpu.VMEM((2, 4, pad, wide), f32),
            pltpu.VMEM((4, count, wide), f32),
            pltpu.VMEM((rows, narrow), f32),
            pltpu.VMEM((2, rows, wide), f32),
            pltpu.VMEM((2, rows, wide), f32),
            pltpu.VMEM((bodies, rows, wide), bf16),
            pltpu.VMEM((rows, wide), f32),
            dma((3,)),
            dma((2,)),
            dma((2,)),
            dma((bodies,)),
            dma((bodies,)),
            pltpu.SemaphoreType.REGULAR,
        ],
        compiler_params=pltpu.CompilerParams(
            collective_id=0,
            has_side_effects=True,
            vmem_limit_bytes=2 * tile_bytes if 2 * tile_bytes < 2**24 else 60 * 2**20,
        ),
    )(*(stay(v) for v in (slip, jnp.swapaxes(inverse, 0, 1), jnp.swapaxes(positions, 0, 1))))
    return pl.pallas_call(
        finish,
        out_shape=(jax.ShapeDtypeStruct(slip.shape, f32),) * 2,
        in_specs=[vmem, vmem],
        out_specs=(pl.BlockSpec(memory_space=pltpu.HBM),) * 2,
        scratch_shapes=[dma((2,))],
        compiler_params=pltpu.CompilerParams(vmem_limit_bytes=2**20),
    )(updated, residual)


def solution(mesh):
    in_specs = (
        P(("groups", "row", "col"), None, None),
        P(("groups", "row", "col"), None, None),
        P("groups", None, None),
    )
    out_specs = (P(("groups", "row", "col"), None, None), P(("groups", "row", "col"), None, None))
    return jax.shard_map(local, mesh=mesh, in_specs=in_specs, out_specs=out_specs, check_vma=False)
```

profile of v0, /device:TPU:0, one launch (start us, length us, event | category | flops | bytes accessed | tf_op | source)
XLA Modules:
  0.0 13.3 jit_solution(14428897129993347554)
XLA Ops:
  0.6 12.0 %shard_map.50 = (f32[1,16,243]{2,1,0:T(8,128)S(1)}, f32[1,16,243]{2,1,0:T(8,128)S(1)}) custom-call(f32[1,16,243]{2,1,0:T(8,128)} %slip_hbm.1, f32[486,1,243]{2,1,0:T(1,128)} %bitcast.2, f32[3,16,81]{2,1,0:T(8,128)} %bitcast.3), custom_call_target="tpu_custom_call" | custom-call | tf_op jit(solution)/shard_map/pallas_call | solution.py:314
  12.6 0.6 %shard_map.51 = (f32[1,16,243]{2,1,0:T(8,128)}, f32[1,16,243]{2,1,0:T(8,128)}) custom-call(f32[1,16,243]{2,1,0:T(8,128)S(1)} %get-tuple-element.4.updated, f32[1,16,243]{2,1,0:T(8,128)S(1)} %get-tuple-element.5.residual), custom_call_target="tpu_custom_call" | custom-call | tf_op jit(solution)/shard_map/pallas_call | solution.py:350
where the time goes:
time: 13.4 us; the launch traced here: 13.3 us
  Pallas kernels  12.6 us (94%)
  between operations  0.64 us (5%)
    pallas_call x1, Pallas kernels, local(): pl.pallas_call(functools.partial(kernel, row_count, col_count, blobs), ou...  12 us
    pallas_call x1, Pallas kernels, local(): pl.pallas_call(finish, out_shape=(jax.ShapeDtypeStruct(slip.shape, f32),)...  0.63 us

commit v1 on v0

v1 whole, which is shorter than its diff:
```python
import functools

import jax
import jax.numpy as jnp
from jax import lax
from jax.experimental import pallas as pl
from jax.experimental.pallas import tpu as pltpu
from jax.sharding import PartitionSpec as P

MESH = pl.DeviceIdType.MESH
LANES = 128
CHUNK = 16
EXTRA = 3


def round_up(value, step):
    return -(-value // step) * step


def split(value):
    high = value.astype(jnp.bfloat16)
    low = (value - high.astype(jnp.float32)).astype(jnp.bfloat16)
    return high, low


def triple(rows, blobs):
    lane = lax.broadcasted_iota(jnp.int32, rows.shape, rows.ndim - 1)
    axis = rows.ndim - 1
    once = pltpu.roll(rows, blobs, axis)
    twice = pltpu.roll(rows, 2 * blobs, axis)
    return jnp.where(lane < blobs, rows, jnp.where(lane < 2 * blobs, once, twice))


def kernel(
    row_count, col_count, blobs, extra,
    slip_hbm, inverse_hbm, positions_hbm,
    updated, residual,
    slip, inverse, positions,
    inv_high, inv_low, tiles, own_rows, own, source, other_slip, part, other_part,
    forces, cross_forces, held, base, far_part, turned, last,
    load_sems, slip_sems, part_sems, send_sems, recv_sems, cross_sems,
    go, ready,
):
    bodies = row_count * col_count // 2
    row = lax.axis_index("row")
    col = lax.axis_index("col")
    half = lax.rem(col, 2)
    partner = col + 1 - 2 * half
    body = (row * col_count + col) // 2
    narrow = 3 * blobs
    wide = source.shape[-1]
    pad = own.shape[2]
    low_side = body < bodies // 2
    lead = body == 0

    def far(step):
        return jnp.where(low_side, bodies - 1 - step, step)

    def same(j):
        there = 2 * j + half
        return {"row": there // col_count, "col": lax.rem(there, col_count)}

    def cross(j):
        there = 2 * j + 1 - half
        return {"row": there // col_count, "col": lax.rem(there, col_count)}

    def loop(start, stop, action):
        def visit(j, carry):
            action(j)
            return carry

        lax.fori_loop(start, stop, visit, 0)

    def signal(sem, device):
        pl.semaphore_signal(sem, inc=1, device_id=device, device_id_type=MESH)

    barrier = pltpu.get_barrier_semaphore()

    @pl.when(half == 0)
    def _():
        signal(barrier, {"col": partner})

    loads = [
        pltpu.make_async_copy(inverse_hbm.at[:, 0, :], inverse, load_sems.at[0]),
        pltpu.make_async_copy(slip_hbm.at[0], slip, load_sems.at[1]),
        pltpu.make_async_copy(positions_hbm, positions, load_sems.at[2]),
    ]
    for load in loads:
        load.start()

    def swap(source_ref, target_ref, sems):
        return pltpu.make_async_remote_copy(
            src_ref=source_ref,
            dst_ref=target_ref,
            send_sem=sems.at[0],
            recv_sem=sems.at[1],
            device_id={"col": partner},
            device_id_type=MESH,
        )

    slip_swap = swap(slip_hbm.at[0], other_slip, slip_sems)

    def first(j):
        there = 2 * j
        return {"row": there // col_count, "col": lax.rem(there, col_count)}

    @pl.when(half == 1)
    def _():
        pl.semaphore_wait(barrier, jnp.where(lead, 1, 3))
        signal(go.at[0], {"col": partner})
        slip_swap.start()

    def greet(j):
        there = 2 * j + jnp.where(lead, 1, 0)
        signal(barrier, {"row": there // col_count, "col": lax.rem(there, col_count)})

    loop(body + 1, bodies, greet)

    @pl.when(half == 0)
    def _():
        pl.semaphore_wait(go.at[0], 1)
        slip_swap.start()

    @pl.when(jnp.logical_not(lead))
    def _():
        signal(ready.at[body], same(0))

        @pl.when((half == 0) & (body > 1))
        def _():
            pl.semaphore_wait(barrier, 2 * (body - 1))

        @pl.when(half == 0)
        def _():
            signal(go.at[1], {"col": partner})

    inv_high[...] = jnp.zeros_like(inv_high)
    inv_low[...] = jnp.zeros_like(inv_low)
    own_rows[...] = jnp.zeros_like(own_rows)

    def build(step, carry):
        j = step // 2
        t = lax.rem(step, 2)
        block = jnp.where(j < bodies, 2 * j + half, 2 * (2 * bodies - 1 - j) + 1 - half)
        lane = lax.broadcasted_iota(jnp.int32, (CHUNK, wide), 1)
        masks = [(lane >= a * blobs) & (lane < (a + 1) * blobs) for a in range(3)]
        there = [
            jnp.broadcast_to(source[a, pl.ds(block, 1), :], (CHUNK, wide)) for a in range(4)
        ]
        for at in range(0, pad, CHUNK):
            d0, d1, d2, db = [own[t, a, at : at + CHUNK, :] - there[a] for a in range(4)]
            dist_sq = d0 * d0 + d1 * d1 + d2 * d2
            r = lax.rsqrt(jnp.where(dist_sq > 0.0, dist_sq, 1.0))
            r2 = r * r
            k = 0.75 * r
            u = k * r2
            apart = dist_sq >= 4.0
            isotropic = jnp.where(
                apart, k + (2.0 / 3.0) * u, 1.0 - (9.0 / 32.0) * (dist_sq * r)
            )
            anisotropic = jnp.where(apart, u - (2.0 * u) * r2, (3.0 / 32.0) * r)
            scaled = anisotropic * db
            for a, da in enumerate((d0, d1, d2)):
                value = scaled * da + jnp.where(masks[a], isotropic, 0.0)
                tiles[j, t, a * pad + at : a * pad + at + CHUNK, :] = value.astype(jnp.bfloat16)
        return carry

    def apply(values, h):
        high, low = split(jnp.pad(values, ((0, 0), (0, wide - narrow))))
        big = inv_high[h]
        small = inv_low[h]
        rows = values.shape[0]
        both = jnp.dot(
            jnp.concatenate([high, low], axis=0), big, preferred_element_type=jnp.float32
        )
        cross = jnp.dot(high, small, preferred_element_type=jnp.float32)
        return both[:rows] + (both[rows:] + cross)

    @pl.when(jnp.logical_not(lead) & (half == 1))
    def _():
        pl.semaphore_wait(go.at[1], 1)

    loop(1, body, lambda j: signal(ready.at[body], same(j)))

    loads[0].wait()
    for h in range(2):
        high, low = split(inverse[h * narrow : (h + 1) * narrow, :])
        inv_high[h, :narrow, :narrow] = high
        inv_low[h, :narrow, :narrow] = low
    loads[1].wait()
    force = apply(slip[...], half)
    slip_swap.wait_recv()
    force = force + apply(other_slip[...], 1 - half)
    forces[body] = force.astype(jnp.bfloat16)
    held[...] = force

    def send(j):
        return pltpu.make_async_remote_copy(
            src_ref=forces.at[body],
            dst_ref=forces.at[body],
            send_sem=send_sems.at[j],
            recv_sem=recv_sems.at[body],
            device_id=same(j),
            device_id_type=MESH,
        )

    slot = bodies - 1 - body
    doubled = (slot < extra) & jnp.logical_not(lead)

    def cross_send():
        return pltpu.make_async_remote_copy(
            src_ref=forces.at[body],
            dst_ref=cross_forces.at[slot],
            send_sem=cross_sems.at[extra],
            recv_sem=cross_sems.at[slot],
            device_id=cross(0),
            device_id_type=MESH,
        )

    @pl.when(jnp.logical_not(lead))
    def _():
        send(0).start()

    @pl.when(doubled)
    def _():
        cross_send().start()

    loop(1, body, lambda j: send(j).start())

    loads[2].wait()
    lane = lax.broadcasted_iota(jnp.int32, source.shape[1:], 1)
    spread = []
    for a in range(3):
        rows = jnp.pad(positions[a], ((0, 0), (0, wide - blobs)))
        spread.append(triple(rows, blobs))
        source[a] = spread[a]
        for t in range(2):
            own_rows[3 * t + a : 3 * t + a + 1, :blobs] = positions[a, pl.ds(2 * body + t, 1), :]
    source[3] = jnp.where(
        lane < blobs, spread[0], jnp.where(lane < 2 * blobs, spread[1], spread[2])
    )
    own_cols = own_rows[...].T
    lane = lax.broadcasted_iota(jnp.int32, (pad, wide), 1)
    for t in range(2):
        cols = [
            jnp.broadcast_to(own_cols[:pad, 3 * t + a : 3 * t + a + 1], (pad, wide))
            for a in range(3)
        ]
        for a in range(3):
            own[t, a] = cols[a]
        own[t, 3] = jnp.where(lane < blobs, cols[0], jnp.where(lane < 2 * blobs, cols[1], cols[2]))

    count = jnp.where(lead, 2 * (bodies + extra), 2 * bodies)
    cut = jnp.where(lead, count, bodies)
    lax.fori_loop(0, cut, build, 0)

    def send_on(j):
        pl.semaphore_wait(ready.at[j], 1)
        send(j).start()

    loop(body + 1, bodies, send_on)
    lax.fori_loop(cut, count, build, 0)

    def product(values, j):
        return lax.dot_general(
            values,
            tiles[j].reshape(6 * pad, wide),
            (((1,), (1,)), ((), ())),
            preferred_element_type=jnp.float32,
        )

    def receive(j):
        pltpu.make_async_remote_copy(
            src_ref=forces.at[j],
            dst_ref=forces.at[j],
            send_sem=send_sems.at[0],
            recv_sem=recv_sems.at[j],
            device_id={"col": partner},
            device_id_type=MESH,
        ).wait_recv()

    def cross_receive(f):
        pltpu.make_async_remote_copy(
            src_ref=cross_forces.at[f],
            dst_ref=cross_forces.at[f],
            send_sem=cross_sems.at[extra],
            recv_sem=cross_sems.at[f],
            device_id={"col": partner},
            device_id_type=MESH,
        ).wait_recv()

    def gather(picks):
        for j in picks:

            @pl.when(j != body)
            def _(j=j):
                receive(j)

        total = product(forces[picks[0]], picks[0])
        for j in picks[1:]:
            total = total + product(forces[j], j)
        return total

    def gather_run(start, stop):
        if stop - start <= 8:
            size = (stop - start + 1) // 2
            total = gather([far(bodies - 1 - k) for k in range(start, start + size)])
            return total + gather([far(bodies - 1 - k) for k in range(start + size, stop)])
        return lax.fori_loop(
            start,
            stop,
            lambda k, total: total + gather([far(bodies - 1 - k)]),
            jnp.zeros((slip.shape[0], 6 * pad), jnp.float32),
        )

    def compact(total):
        full = round_up(6 * pad, LANES)
        total = jnp.pad(total, ((0, 0), (0, full - 6 * pad)))
        lane = lax.broadcasted_iota(jnp.int32, total.shape, 1)

        def moved(by):
            return pltpu.roll(total, full - by, 1) if by else total

        values = []
        for t in range(2):
            start = 3 * t * pad
            shift = pad - blobs
            value = jnp.where(
                lane < blobs,
                moved(start),
                jnp.where(lane < 2 * blobs, moved(start + shift), moved(start + 2 * shift)),
            )
            values.append(value[:, :wide])
        return values

    part_swap = swap(part, other_part, part_sems)

    def share(total):
        for t, value in enumerate(compact(total)):
            part[t] = value
        part_swap.start()

    def settle(more):
        part_swap.wait()
        sums = [part[t] + other_part[t] for t in (half, 1 - half)]
        if more:
            sums = [value + far_part[t] for value, t in zip(sums, (half, 1 - half))]
        mine = slip[...] - sums[0][:, :narrow]
        theirs = other_slip[...] - sums[1][:, :narrow]
        return mine, held[...] + (apply(mine, half) + apply(theirs, 1 - half))

    @pl.when(jnp.logical_not(lead))
    def _():
        share(gather_run(0, bodies))
        mine, result = settle(False)
        residual[0] = mine
        updated[0] = result[:, :narrow]

    @pl.when(lead)
    def _():
        row_at = lax.broadcasted_iota(jnp.int32, (wide, 3 * pad), 0)
        col_at = lax.broadcasted_iota(jnp.int32, (wide, 3 * pad), 1)
        gap = pad - blobs
        wanted = row_at + jnp.where(row_at < blobs, 0, jnp.where(row_at < 2 * blobs, gap, 2 * gap))
        picked = jnp.where((col_at == wanted) & (row_at < narrow), 1.0, 0.0).astype(jnp.bfloat16)
        for s, block in enumerate((bodies - 1, bodies)):
            lanes = slice(s * wide, (s + 1) * wide)
            folded = jnp.zeros((wide, wide), jnp.float32)
            for t in range(2):
                tight = jnp.dot(picked, tiles[block, t], preferred_element_type=jnp.float32)
                tight = tight.astype(jnp.bfloat16)
                turned[t] = tight
                for side in (inv_high, inv_low):
                    folded = folded + lax.dot_general(
                        side[t], tight, (((0,), (0,)), ((), ())), preferred_element_type=jnp.float32
                    )
            high, low = split(folded)
            last[:wide, lanes] = turned[half]
            last[wide : 2 * wide, lanes] = high
            last[2 * wide :, lanes] = low

        share(gather_run(0, bodies - extra))

        if extra > 1:
            for f in range(1, extra):
                receive(bodies - 1 - f)
                cross_receive(f)
            total = jnp.zeros((slip.shape[0], 6 * pad), jnp.float32)
            for f in range(1, extra):
                total = total + product(forces[bodies - 1 - f], bodies - 1 - f)
                total = total + product(cross_forces[f], bodies + f)
            for t, value in enumerate(compact(total)):
                far_part[t] = value

        mine, result = settle(extra > 1)
        base[...] = mine
        held[...] = result

        receive(bodies - 1)
        cross_receive(0)
        final = lax.dot_general(
            jnp.concatenate([forces[bodies - 1], cross_forces[0]], axis=1),
            last[...],
            (((1,), (1,)), ((), ())),
            preferred_element_type=jnp.float32,
        )
        residual[0] = base[...] - final[:, :narrow]
        change = final[:, wide : 2 * wide] + final[:, 2 * wide :]
        updated[0] = (held[...] - change)[:, :narrow]

    def sent(j):
        send(j).wait_send()

    loop(0, body, sent)
    loop(body + 1, bodies, sent)

    @pl.when(doubled)
    def _():
        cross_send().wait_send()

    slip_swap.wait_send()


def finish(updated, residual, updated_out, residual_out, sems):
    copies = [
        pltpu.make_async_copy(updated, updated_out, sems.at[0]),
        pltpu.make_async_copy(residual, residual_out, sems.at[1]),
    ]
    for copy in copies:
        copy.start()
    for copy in copies:
        copy.wait()


def stay(value):
    return pltpu.with_memory_space_constraint(value, pltpu.HBM)


def local(slip, inverse, positions):
    row_count = lax.axis_size("row")
    col_count = lax.axis_size("col")
    count = row_count * col_count
    bodies = count // 2
    blobs = positions.shape[2]
    rows, narrow = slip.shape[1:]
    wide = round_up(narrow, LANES)
    pad = round_up(blobs, CHUNK)
    vmem = pl.BlockSpec(memory_space=pltpu.VMEM)
    f32, bf16 = jnp.float32, jnp.bfloat16
    dma = pltpu.SemaphoreType.DMA
    extra = min(EXTRA, bodies // 2)
    tile_bytes = (bodies + extra) * 6 * pad * wide * 2
    updated, residual = pl.pallas_call(
        functools.partial(kernel, row_count, col_count, blobs, extra),
        out_shape=(
            pltpu.VMEM(slip.shape, f32),
            pltpu.VMEM(slip.shape, f32),
        ),
        in_specs=[pl.BlockSpec(memory_space=pltpu.HBM)] * 3,
        out_specs=(vmem, vmem),
        scratch_shapes=[
            pltpu.VMEM((rows, narrow), f32),
            pltpu.VMEM(inverse.shape[1:], f32),
            pltpu.VMEM((3, count, blobs), f32),
            pltpu.VMEM((2, wide, wide), bf16),
            pltpu.VMEM((2, wide, wide), bf16),
            pltpu.VMEM((bodies + extra, 2, 3 * pad, wide), bf16),
            pltpu.VMEM((8, LANES), f32),
            pltpu.VMEM((2, 4, pad, wide), f32),
            pltpu.VMEM((4, count, wide), f32),
            pltpu.VMEM((rows, narrow), f32),
            pltpu.VMEM((2, rows, wide), f32),
            pltpu.VMEM((2, rows, wide), f32),
            pltpu.VMEM((bodies, rows, wide), bf16),
            pltpu.VMEM((extra, rows, wide), bf16),
            pltpu.VMEM((rows, wide), f32),
            pltpu.VMEM((rows, narrow), f32),
            pltpu.VMEM((2, rows, wide), f32),
            pltpu.VMEM((2, wide, wide), bf16),
            pltpu.VMEM((3 * wide, 2 * wide), bf16),
            dma((3,)),
            dma((2,)),
            dma((2,)),
            dma((bodies,)),
            dma((bodies,)),
            dma((extra + 1,)),
            pltpu.SemaphoreType.REGULAR((2,)),
            pltpu.SemaphoreType.REGULAR((bodies,)),
        ],
        compiler_params=pltpu.CompilerParams(
            collective_id=0,
            has_side_effects=True,
            vmem_limit_bytes=min(tile_bytes + 16 * 2**20, 60 * 2**20),
        ),
    )(*(stay(v) for v in (slip, jnp.swapaxes(inverse, 0, 1), jnp.swapaxes(positions, 0, 1))))
    return pl.pallas_call(
        finish,
        out_shape=(jax.ShapeDtypeStruct(slip.shape, f32),) * 2,
        in_specs=[vmem, vmem],
        out_specs=(pl.BlockSpec(memory_space=pltpu.HBM),) * 2,
        scratch_shapes=[dma((2,))],
        compiler_params=pltpu.CompilerParams(vmem_limit_bytes=2**20),
    )(updated, residual)


def solution(mesh):
    in_specs = (
        P(("groups", "row", "col"), None, None),
        P(("groups", "row", "col"), None, None),
        P("groups", None, None),
    )
    out_specs = (P(("groups", "row", "col"), None, None), P(("groups", "row", "col"), None, None))
    return jax.shard_map(local, mesh=mesh, in_specs=in_specs, out_specs=out_specs, check_vma=False)
```

time: 13.4 us -> 12.2 us (0.910)
  Pallas kernels: 12.6 us -> 11.4 us
    pallas_call x1, Pallas kernels: 12 us -> 10.8 us  [local(): pl.pallas_call(functools.partial(kernel, row_count, col_count, blobs, ext...]
where the time goes in v1:
time: 12.2 us; the launch traced here: 12.1 us
  Pallas kernels  11.4 us (93%)
  between operations  0.64 us (5%)
    pallas_call x1, Pallas kernels, local(): pl.pallas_call(functools.partial(kernel, row_count, col_count, blobs, ext...  10.8 us
    pallas_call x1, Pallas kernels, local(): pl.pallas_call(finish, out_shape=(jax.ShapeDtypeStruct(slip.shape, f32),)...  0.63 us

profile of v1, /device:TPU:0, one launch (start us, length us, event | category | flops | bytes accessed | tf_op | source)
XLA Modules:
  0.0 12.1 jit_solution(137114429914376394)
XLA Ops:
  0.6 10.8 %shard_map.50 = (f32[1,16,243]{2,1,0:T(8,128)S(1)}, f32[1,16,243]{2,1,0:T(8,128)S(1)}) custom-call(f32[1,16,243]{2,1,0:T(8,128)} %slip_hbm.1, f32[486,1,243]{2,1,0:T(1,128)} %bitcast.2, f32[3,16,81]{2,1,0:T(8,128)} %bitcast.3), custom_call_target="tpu_custom_call" | custom-call | tf_op jit(solution)/shard_map/pallas_call | solution.py:452
  11.4 0.6 %shard_map.51 = (f32[1,16,243]{2,1,0:T(8,128)}, f32[1,16,243]{2,1,0:T(8,128)}) custom-call(f32[1,16,243]{2,1,0:T(8,128)S(1)} %get-tuple-element.4.updated, f32[1,16,243]{2,1,0:T(8,128)S(1)} %get-tuple-element.5.residual), custom_call_target="tpu_custom_call" | custom-call | tf_op jit(solution)/shard_map/pallas_call | solution.py:495

commit v2 on v1

--- a/solution.py
+++ b/solution.py
@@ -21,14 +21,6 @@
     high = value.astype(jnp.bfloat16)
     low = (value - high.astype(jnp.float32)).astype(jnp.bfloat16)
     return high, low
-
-
-def triple(rows, blobs):
-    lane = lax.broadcasted_iota(jnp.int32, rows.shape, rows.ndim - 1)
-    axis = rows.ndim - 1
-    once = pltpu.roll(rows, blobs, axis)
-    twice = pltpu.roll(rows, 2 * blobs, axis)
-    return jnp.where(lane < blobs, rows, jnp.where(lane < 2 * blobs, once, twice))
 
 
 def kernel(
@@ -48,7 +40,7 @@
     partner = col + 1 - 2 * half
     body = (row * col_count + col) // 2
     narrow = 3 * blobs
-    wide = source.shape[-1]
+    wide = inv_high.shape[-1]
     pad = own.shape[2]
     low_side = body < bodies // 2
     lead = body == 0
@@ -76,7 +68,7 @@
 
     barrier = pltpu.get_barrier_semaphore()
 
-    @pl.when(half == 0)
+    @pl.when(half == 1)
     def _():
         signal(barrier, {"col": partner})
 
@@ -104,19 +96,23 @@
         there = 2 * j
         return {"row": there // col_count, "col": lax.rem(there, col_count)}
 
-    @pl.when(half == 1)
+    @pl.when(half == 0)
     def _():
         pl.semaphore_wait(barrier, jnp.where(lead, 1, 3))
         signal(go.at[0], {"col": partner})
         slip_swap.start()
 
     def greet(j):
-        there = 2 * j + jnp.where(lead, 1, 0)
+        there = 2 * j + jnp.where(lead, 0, 1)
         signal(barrier, {"row": there // col_count, "col": lax.rem(there, col_count)})
 
-    loop(body + 1, bodies, greet)
-
-    @pl.when(half == 0)
+    def others(action):
+        loop(1, body, action)
+        loop(body + 1, bodies, action)
+
+    others(greet)
+
+    @pl.when(half == 1)
     def _():
         pl.semaphore_wait(go.at[0], 1)
         slip_swap.start()
@@ -124,14 +120,6 @@
     @pl.when(jnp.logical_not(lead))
     def _():
         signal(ready.at[body], same(0))
-
-        @pl.when((half == 0) & (body > 1))
-        def _():
-            pl.semaphore_wait(barrier, 2 * (body - 1))
-
-        @pl.when(half == 0)
-        def _():
-            signal(go.at[1], {"col": partner})
 
     inv_high[...] = jnp.zeros_like(inv_high)
     inv_low[...] = jnp.zeros_like(inv_low)
@@ -141,14 +129,23 @@
         j = step // 2
         t = lax.rem(step, 2)
         block = jnp.where(j < bodies, 2 * j + half, 2 * (2 * bodies - 1 - j) + 1 - half)
-        lane = lax.broadcasted_iota(jnp.int32, (CHUNK, wide), 1)
-        masks = [(lane >= a * blobs) & (lane < (a + 1) * blobs) for a in range(3)]
+        lane = lax.broadcasted_iota(jnp.int32, (CHUNK, LANES), 1)
         there = [
-            jnp.broadcast_to(source[a, pl.ds(block, 1), :], (CHUNK, wide)) for a in range(4)
+            jnp.broadcast_to(source[a, pl.ds(block, 1), :], (CHUNK, LANES)) for a in range(3)
         ]
+
+        def spread(parts, group):
+            value = None
+            for b, part_b in enumerate(parts):
+                start = b * blobs - group * LANES
+                if start >= LANES or start + blobs <= 0:
+                    continue
+                value = part_b if value is None else jnp.where(lane < start, value, part_b)
+            return value
+
         for at in range(0, pad, CHUNK):
-            d0, d1, d2, db = [own[t, a, at : at + CHUNK, :] - there[a] for a in range(4)]
-            dist_sq = d0 * d0 + d1 * d1 + d2 * d2
+            d = [own[t, a, at : at + CHUNK, :] - there[a] for a in range(3)]
+            dist_sq = d[0] * d[0] + d[1] * d[1] + d[2] * d[2]
             r = lax.rsqrt(jnp.where(dist_sq > 0.0, dist_sq, 1.0))
             r2 = r * r
             k = 0.75 * r
@@ -158,10 +155,22 @@
                 apart, k + (2.0 / 3.0) * u, 1.0 - (9.0 / 32.0) * (dist_sq * r)
             )
             anisotropic = jnp.where(apart, u - (2.0 * u) * r2, (3.0 / 32.0) * r)
-            scaled = anisotropic * db
-            for a, da in enumerate((d0, d1, d2)):
-                value = scaled * da + jnp.where(masks[a], isotropic, 0.0)
-                tiles[j, t, a * pad + at : a * pad + at + CHUNK, :] = value.astype(jnp.bfloat16)
+            scaled = [anisotropic * da for da in d]
+            for a in range(3):
+                parts = []
+                for b in range(3):
+                    value = scaled[min(a, b)] * d[max(a, b)]
+                    if a == b:
+                        value = value + isotropic
+                    shift = b * blobs % LANES
+                    parts.append(pltpu.roll(value, shift, 1) if shift else value)
+                for group in range(wide // LANES):
+                    tiles[
+                        j,
+                        t,
+                        a * pad + at : a * pad + at + CHUNK,
+                        group * LANES : (group + 1) * LANES,
+                    ] = spread(parts, group).astype(jnp.bfloat16)
         return carry
 
     def apply(values, h):
@@ -174,12 +183,6 @@
         )
         cross = jnp.dot(high, small, preferred_element_type=jnp.float32)
         return both[:rows] + (both[rows:] + cross)
-
-    @pl.when(jnp.logical_not(lead) & (half == 1))
-    def _():
-        pl.semaphore_wait(go.at[1], 1)
-
-    loop(1, body, lambda j: signal(ready.at[body], same(j)))
 
     loads[0].wait()
     for h in range(2):
@@ -224,41 +227,42 @@
     def _():
         cross_send().start()
 
-    loop(1, body, lambda j: send(j).start())
+    if bodies > 2:
+
+        @pl.when(jnp.logical_not(lead) & (half == 1))
+        def _():
+            pl.semaphore_wait(barrier, 2 * (bodies - 2))
+            signal(go.at[1], {"col": partner})
+
+        @pl.when(jnp.logical_not(lead) & (half == 0))
+        def _():
+            pl.semaphore_wait(go.at[1], 1)
+
+    @pl.when(jnp.logical_not(lead))
+    def _():
+        others(lambda j: send(j).start())
 
     loads[2].wait()
-    lane = lax.broadcasted_iota(jnp.int32, source.shape[1:], 1)
-    spread = []
     for a in range(3):
-        rows = jnp.pad(positions[a], ((0, 0), (0, wide - blobs)))
-        spread.append(triple(rows, blobs))
-        source[a] = spread[a]
+        source[a] = jnp.pad(positions[a], ((0, 0), (0, LANES - blobs)))
         for t in range(2):
             own_rows[3 * t + a : 3 * t + a + 1, :blobs] = positions[a, pl.ds(2 * body + t, 1), :]
-    source[3] = jnp.where(
-        lane < blobs, spread[0], jnp.where(lane < 2 * blobs, spread[1], spread[2])
-    )
     own_cols = own_rows[...].T
-    lane = lax.broadcasted_iota(jnp.int32, (pad, wide), 1)
     for t in range(2):
-        cols = [
-            jnp.broadcast_to(own_cols[:pad, 3 * t + a : 3 * t + a + 1], (pad, wide))
-            for a in range(3)
-        ]
         for a in range(3):
-            own[t, a] = cols[a]
-        own[t, 3] = jnp.where(lane < blobs, cols[0], jnp.where(lane < 2 * blobs, cols[1], cols[2]))
-
-    count = jnp.where(lead, 2 * (bodies + extra), 2 * bodies)
-    cut = jnp.where(lead, count, bodies)
-    lax.fori_loop(0, cut, build, 0)
+            own[t, a] = jnp.broadcast_to(
+                own_cols[:pad, 3 * t + a : 3 * t + a + 1], (pad, LANES)
+            )
+
+    lax.fori_loop(0, jnp.where(lead, 2 * (bodies + extra), 2 * bodies), build, 0)
 
     def send_on(j):
         pl.semaphore_wait(ready.at[j], 1)
         send(j).start()
 
-    loop(body + 1, bodies, send_on)
-    lax.fori_loop(cut, count, build, 0)
+    @pl.when(lead)
+    def _():
+        loop(1, bodies, send_on)
 
     def product(values, j):
         return lax.dot_general(
@@ -465,8 +469,8 @@
             pltpu.VMEM((2, wide, wide), bf16),
             pltpu.VMEM((bodies + extra, 2, 3 * pad, wide), bf16),
             pltpu.VMEM((8, LANES), f32),
-            pltpu.VMEM((2, 4, pad, wide), f32),
-            pltpu.VMEM((4, count, wide), f32),
+            pltpu.VMEM((2, 3, pad, LANES), f32),
+            pltpu.VMEM((3, count, LANES), f32),
             pltpu.VMEM((rows, narrow), f32),
             pltpu.VMEM((2, rows, wide), f32),
             pltpu.VMEM((2, rows, wide), f32),

time: 12.2 us -> 11.8 us (0.967)
  the two profiles are of different devices: /device:TPU:0 before, /device:TPU:7 now
where the time goes in v2:
time: 11.8 us; the launch traced here: 11.6 us
  Pallas kernels  11 us (93%)
  between operations  0.64 us (5%)
    pallas_call x1, Pallas kernels, local(): pl.pallas_call(functools.partial(kernel, row_count, col_count, blobs, ext...  10.4 us
    pallas_call x1, Pallas kernels, local(): pl.pallas_call(finish, out_shape=(jax.ShapeDtypeStruct(slip.shape, f32),)...  0.63 us

profile of v2, /device:TPU:7, one launch (start us, length us, event | category | flops | bytes accessed | tf_op | source)
XLA Modules:
  0.0 11.6 jit_solution(2079936575202116756)
XLA Ops:
  0.6 10.4 %shard_map.50 = (f32[1,16,243]{2,1,0:T(8,128)S(1)}, f32[1,16,243]{2,1,0:T(8,128)S(1)}) custom-call(f32[1,16,243]{2,1,0:T(8,128)} %slip_hbm.1, f32[486,1,243]{2,1,0:T(1,128)} %bitcast.2, f32[3,16,81]{2,1,0:T(8,128)} %bitcast.3), custom_call_target="tpu_custom_call" | custom-call | tf_op jit(solution)/shard_map/pallas_call | solution.py:456
  11.0 0.6 %shard_map.51 = (f32[1,16,243]{2,1,0:T(8,128)}, f32[1,16,243]{2,1,0:T(8,128)}) custom-call(f32[1,16,243]{2,1,0:T(8,128)S(1)} %get-tuple-element.4.updated, f32[1,16,243]{2,1,0:T(8,128)S(1)} %get-tuple-element.5.residual), custom_call_target="tpu_custom_call" | custom-call | tf_op jit(solution)/shard_map/pallas_call | solution.py:499

commit v3 on v2

--- a/solution.py
+++ b/solution.py
@@ -29,8 +29,8 @@
     updated, residual,
     slip, inverse, positions,
     inv_high, inv_low, tiles, own_rows, own, source, other_slip, part, other_part,
-    forces, cross_forces, held, base, far_part, turned, last,
-    load_sems, slip_sems, part_sems, send_sems, recv_sems, cross_sems,
+    forces, twin_forces, held, base, far_part, turned, last,
+    load_sems, slip_sems, part_sems, send_sems, recv_sems, twin_sems,
     go, ready,
 ):
     bodies = row_count * col_count // 2
@@ -68,18 +68,6 @@
 
     barrier = pltpu.get_barrier_semaphore()
 
-    @pl.when(half == 1)
-    def _():
-        signal(barrier, {"col": partner})
-
-    loads = [
-        pltpu.make_async_copy(inverse_hbm.at[:, 0, :], inverse, load_sems.at[0]),
-        pltpu.make_async_copy(slip_hbm.at[0], slip, load_sems.at[1]),
-        pltpu.make_async_copy(positions_hbm, positions, load_sems.at[2]),
-    ]
-    for load in loads:
-        load.start()
-
     def swap(source_ref, target_ref, sems):
         return pltpu.make_async_remote_copy(
             src_ref=source_ref,
@@ -92,9 +80,9 @@
 
     slip_swap = swap(slip_hbm.at[0], other_slip, slip_sems)
 
-    def first(j):
-        there = 2 * j
-        return {"row": there // col_count, "col": lax.rem(there, col_count)}
+    @pl.when(half == 1)
+    def _():
+        signal(barrier, {"col": partner})
 
     @pl.when(half == 0)
     def _():
@@ -102,6 +90,14 @@
         signal(go.at[0], {"col": partner})
         slip_swap.start()
 
+    loads = [
+        pltpu.make_async_copy(inverse_hbm.at[:, 0, :], inverse, load_sems.at[0]),
+        pltpu.make_async_copy(slip_hbm.at[0], slip, load_sems.at[1]),
+        pltpu.make_async_copy(positions_hbm, positions, load_sems.at[2]),
+    ]
+    for load in (loads[1], loads[0], loads[2]):
+        load.start()
+
     def greet(j):
         there = 2 * j + jnp.where(lead, 0, 1)
         signal(barrier, {"row": there // col_count, "col": lax.rem(there, col_count)})
@@ -114,21 +110,22 @@
 
     @pl.when(half == 1)
     def _():
+        loads[1].wait()
         pl.semaphore_wait(go.at[0], 1)
-        slip_swap.start()
+        swap(slip, other_slip, slip_sems).start()
 
     @pl.when(jnp.logical_not(lead))
     def _():
-        signal(ready.at[body], same(0))
+        signal(ready.at[body], cross(0))
 
     inv_high[...] = jnp.zeros_like(inv_high)
     inv_low[...] = jnp.zeros_like(inv_low)
     own_rows[...] = jnp.zeros_like(own_rows)
 
     def build(step, carry):
-        j = step // 2
-        t = lax.rem(step, 2)
-        block = jnp.where(j < bodies, 2 * j + half, 2 * (2 * bodies - 1 - j) + 1 - half)
+        j = step
+        here = jnp.where(j == body, half, 1 - half)
+        block = jnp.where(j < bodies, 2 * j + here, 2 * (2 * bodies - 1 - j) + half)
         lane = lax.broadcasted_iota(jnp.int32, (CHUNK, LANES), 1)
         there = [
             jnp.broadcast_to(source[a, pl.ds(block, 1), :], (CHUNK, LANES)) for a in range(3)
@@ -143,7 +140,7 @@
                 value = part_b if value is None else jnp.where(lane < start, value, part_b)
             return value
 
-        for at in range(0, pad, CHUNK):
+        for t, at in [(t, at) for at in range(0, pad, CHUNK) for t in range(2)]:
             d = [own[t, a, at : at + CHUNK, :] - there[a] for a in range(3)]
             dist_sq = d[0] * d[0] + d[1] * d[1] + d[2] * d[2]
             r = lax.rsqrt(jnp.where(dist_sq > 0.0, dist_sq, 1.0))
@@ -189,7 +186,10 @@
         high, low = split(inverse[h * narrow : (h + 1) * narrow, :])
         inv_high[h, :narrow, :narrow] = high
         inv_low[h, :narrow, :narrow] = low
-    loads[1].wait()
+    @pl.when(half == 0)
+    def _():
+        loads[1].wait()
+
     force = apply(slip[...], half)
     slip_swap.wait_recv()
     force = force + apply(other_slip[...], 1 - half)
@@ -202,20 +202,20 @@
             dst_ref=forces.at[body],
             send_sem=send_sems.at[j],
             recv_sem=recv_sems.at[body],
-            device_id=same(j),
+            device_id=cross(j),
             device_id_type=MESH,
         )
 
     slot = bodies - 1 - body
     doubled = (slot < extra) & jnp.logical_not(lead)
 
-    def cross_send():
+    def twin_send():
         return pltpu.make_async_remote_copy(
             src_ref=forces.at[body],
-            dst_ref=cross_forces.at[slot],
-            send_sem=cross_sems.at[extra],
-            recv_sem=cross_sems.at[slot],
-            device_id=cross(0),
+            dst_ref=twin_forces.at[slot],
+            send_sem=twin_sems.at[extra],
+            recv_sem=twin_sems.at[slot],
+            device_id=same(0),
             device_id_type=MESH,
         )
 
@@ -225,7 +225,7 @@
 
     @pl.when(doubled)
     def _():
-        cross_send().start()
+        twin_send().start()
 
     if bodies > 2:
 
@@ -254,7 +254,7 @@
                 own_cols[:pad, 3 * t + a : 3 * t + a + 1], (pad, LANES)
             )
 
-    lax.fori_loop(0, jnp.where(lead, 2 * (bodies + extra), 2 * bodies), build, 0)
+    lax.fori_loop(0, jnp.where(lead, bodies + extra, bodies), build, 0)
 
     def send_on(j):
         pl.semaphore_wait(ready.at[j], 1)
@@ -282,12 +282,12 @@
             device_id_type=MESH,
         ).wait_recv()
 
-    def cross_receive(f):
+    def twin_receive(f):
         pltpu.make_async_remote_copy(
-            src_ref=cross_forces.at[f],
-            dst_ref=cross_forces.at[f],
-            send_sem=cross_sems.at[extra],
-            recv_sem=cross_sems.at[f],
+            src_ref=twin_forces.at[f],
+            dst_ref=twin_forces.at[f],
+            send_sem=twin_sems.at[extra],
+            recv_sem=twin_sems.at[f],
             device_id={"col": partner},
             device_id_type=MESH,
         ).wait_recv()
@@ -367,31 +367,33 @@
         wanted = row_at + jnp.where(row_at < blobs, 0, jnp.where(row_at < 2 * blobs, gap, 2 * gap))
         picked = jnp.where((col_at == wanted) & (row_at < narrow), 1.0, 0.0).astype(jnp.bfloat16)
         for s, block in enumerate((bodies - 1, bodies)):
-            lanes = slice(s * wide, (s + 1) * wide)
+            rows = slice(s * wide, (s + 1) * wide)
             folded = jnp.zeros((wide, wide), jnp.float32)
             for t in range(2):
-                tight = jnp.dot(picked, tiles[block, t], preferred_element_type=jnp.float32)
-                tight = tight.astype(jnp.bfloat16)
+                tight = lax.dot_general(
+                    tiles[block, t],
+                    picked,
+                    (((0,), (1,)), ((), ())),
+                    preferred_element_type=jnp.float32,
+                ).astype(jnp.bfloat16)
                 turned[t] = tight
                 for side in (inv_high, inv_low):
-                    folded = folded + lax.dot_general(
-                        side[t], tight, (((0,), (0,)), ((), ())), preferred_element_type=jnp.float32
-                    )
+                    folded = folded + jnp.dot(tight, side[t], preferred_element_type=jnp.float32)
             high, low = split(folded)
-            last[:wide, lanes] = turned[half]
-            last[wide : 2 * wide, lanes] = high
-            last[2 * wide :, lanes] = low
+            last[rows, :wide] = turned[half]
+            last[rows, wide : 2 * wide] = high
+            last[rows, 2 * wide :] = low
 
         share(gather_run(0, bodies - extra))
 
         if extra > 1:
             for f in range(1, extra):
                 receive(bodies - 1 - f)
-                cross_receive(f)
+                twin_receive(f)
             total = jnp.zeros((slip.shape[0], 6 * pad), jnp.float32)
             for f in range(1, extra):
                 total = total + product(forces[bodies - 1 - f], bodies - 1 - f)
-                total = total + product(cross_forces[f], bodies + f)
+                total = total + product(twin_forces[f], bodies + f)
             for t, value in enumerate(compact(total)):
                 far_part[t] = value
 
@@ -400,11 +402,10 @@
         held[...] = result
 
         receive(bodies - 1)
-        cross_receive(0)
-        final = lax.dot_general(
-            jnp.concatenate([forces[bodies - 1], cross_forces[0]], axis=1),
+        twin_receive(0)
+        final = jnp.dot(
+            jnp.concatenate([forces[bodies - 1], twin_forces[0]], axis=1),
             last[...],
-            (((1,), (1,)), ((), ())),
             preferred_element_type=jnp.float32,
         )
         residual[0] = base[...] - final[:, :narrow]
@@ -419,7 +420,7 @@
 
     @pl.when(doubled)
     def _():
-        cross_send().wait_send()
+        twin_send().wait_send()
 
     slip_swap.wait_send()
 
@@ -480,7 +481,7 @@
             pltpu.VMEM((rows, narrow), f32),
             pltpu.VMEM((2, rows, wide), f32),
             pltpu.VMEM((2, wide, wide), bf16),
-            pltpu.VMEM((3 * wide, 2 * wide), bf16),
+            pltpu.VMEM((2 * wide, 3 * wide), bf16),
             dma((3,)),
             dma((2,)),
             dma((2,)),

time: 11.8 us -> 11.3 us (0.958)
  the two profiles are of different devices: /device:TPU:7 before, /device:TPU:0 now
where the time goes in v3:
time: 11.3 us; the launch traced here: 11.2 us
  Pallas kernels  10.6 us (94%)
  between operations  0.64 us (6%)
    pallas_call x1, Pallas kernels, local(): pl.pallas_call(functools.partial(kernel, row_count, col_count, blobs, ext...  9.93 us
    pallas_call x1, Pallas kernels, local(): pl.pallas_call(finish, out_shape=(jax.ShapeDtypeStruct(slip.shape, f32),)...  0.63 us

profile of v3, /device:TPU:0, one launch (start us, length us, event | category | flops | bytes accessed | tf_op | source)
XLA Modules:
  0.0 11.2 jit_solution(5785439672293350193)
XLA Ops:
  0.6 9.9 %shard_map.50 = (f32[1,16,243]{2,1,0:T(8,128)S(1)}, f32[1,16,243]{2,1,0:T(8,128)S(1)}) custom-call(f32[1,16,243]{2,1,0:T(8,128)} %slip_hbm.1, f32[486,1,243]{2,1,0:T(1,128)} %bitcast.2, f32[3,16,81]{2,1,0:T(8,128)} %bitcast.3), custom_call_target="tpu_custom_call" | custom-call | tf_op jit(solution)/shard_map/pallas_call | solution.py:457
  10.6 0.6 %shard_map.51 = (f32[1,16,243]{2,1,0:T(8,128)}, f32[1,16,243]{2,1,0:T(8,128)}) custom-call(f32[1,16,243]{2,1,0:T(8,128)S(1)} %get-tuple-element.4.updated, f32[1,16,243]{2,1,0:T(8,128)S(1)} %get-tuple-element.5.residual), custom_call_target="tpu_custom_call" | custom-call | tf_op jit(solution)/shard_map/pallas_call | solution.py:500

commit v4 on v3

--- a/solution.py
+++ b/solution.py
@@ -91,11 +91,16 @@
         slip_swap.start()
 
     loads = [
-        pltpu.make_async_copy(inverse_hbm.at[:, 0, :], inverse, load_sems.at[0]),
-        pltpu.make_async_copy(slip_hbm.at[0], slip, load_sems.at[1]),
-        pltpu.make_async_copy(positions_hbm, positions, load_sems.at[2]),
+        pltpu.make_async_copy(slip_hbm.at[0], slip, load_sems.at[0]),
+        pltpu.make_async_copy(positions_hbm, positions, load_sems.at[1]),
     ]
-    for load in (loads[1], loads[0], loads[2]):
+    fetches = [
+        pltpu.make_async_copy(
+            inverse_hbm.at[pl.ds(h * narrow, narrow), 0, :], inverse.at[h], load_sems.at[2 + k]
+        )
+        for k, h in enumerate((half, 1 - half))
+    ]
+    for load in (loads[0], *fetches, loads[1]):
         load.start()
 
     def greet(j):
@@ -110,7 +115,7 @@
 
     @pl.when(half == 1)
     def _():
-        loads[1].wait()
+        loads[0].wait()
         pl.semaphore_wait(go.at[0], 1)
         swap(slip, other_slip, slip_sems).start()
 
@@ -181,18 +186,22 @@
         cross = jnp.dot(high, small, preferred_element_type=jnp.float32)
         return both[:rows] + (both[rows:] + cross)
 
-    loads[0].wait()
-    for h in range(2):
-        high, low = split(inverse[h * narrow : (h + 1) * narrow, :])
+    def prepare(h):
+        high, low = split(inverse[h])
         inv_high[h, :narrow, :narrow] = high
         inv_low[h, :narrow, :narrow] = low
+
+    fetches[0].wait()
+    prepare(half)
+
     @pl.when(half == 0)
     def _():
-        loads[1].wait()
-
-    force = apply(slip[...], half)
+        loads[0].wait()
+
+    fetches[1].wait()
+    prepare(1 - half)
     slip_swap.wait_recv()
-    force = force + apply(other_slip[...], 1 - half)
+    force = apply(slip[...], half) + apply(other_slip[...], 1 - half)
     forces[body] = force.astype(jnp.bfloat16)
     held[...] = force
 
@@ -219,13 +228,13 @@
             device_id_type=MESH,
         )
 
+    @pl.when(doubled)
+    def _():
+        twin_send().start()
+
     @pl.when(jnp.logical_not(lead))
     def _():
         send(0).start()
-
-    @pl.when(doubled)
-    def _():
-        twin_send().start()
 
     if bodies > 2:
 
@@ -242,7 +251,7 @@
     def _():
         others(lambda j: send(j).start())
 
-    loads[2].wait()
+    loads[1].wait()
     for a in range(3):
         source[a] = jnp.pad(positions[a], ((0, 0), (0, LANES - blobs)))
         for t in range(2):
@@ -254,15 +263,21 @@
                 own_cols[:pad, 3 * t + a : 3 * t + a + 1], (pad, LANES)
             )
 
-    lax.fori_loop(0, jnp.where(lead, bodies + extra, bodies), build, 0)
-
     def send_on(j):
         pl.semaphore_wait(ready.at[j], 1)
         send(j).start()
 
+    total_slots = jnp.where(lead, bodies + extra, bodies)
+    early = jnp.where(lead, bodies // 2 - 1, 0)
+    mid = jnp.where(lead, bodies // 2 + 1, 0)
+    lax.fori_loop(0, mid, build, 0)
+    loop(1, early + 1, send_on)
+    lax.fori_loop(mid, total_slots, build, 0)
+
     @pl.when(lead)
     def _():
-        loop(1, bodies, send_on)
+        loop(bodies // 2, bodies, send_on)
+
 
     def product(values, j):
         return lax.dot_general(
@@ -336,6 +351,19 @@
             values.append(value[:, :wide])
         return values
 
+    def sent(j):
+        send(j).wait_send()
+
+    def all_sent():
+        loop(0, body, sent)
+        loop(body + 1, bodies, sent)
+
+        @pl.when(doubled)
+        def _():
+            twin_send().wait_send()
+
+        slip_swap.wait_send()
+
     part_swap = swap(part, other_part, part_sems)
 
     def share(total):
@@ -344,6 +372,7 @@
         part_swap.start()
 
     def settle(more):
+        all_sent()
         part_swap.wait()
         sums = [part[t] + other_part[t] for t in (half, 1 - half)]
         if more:
@@ -411,18 +440,6 @@
         residual[0] = base[...] - final[:, :narrow]
         change = final[:, wide : 2 * wide] + final[:, 2 * wide :]
         updated[0] = (held[...] - change)[:, :narrow]
-
-    def sent(j):
-        send(j).wait_send()
-
-    loop(0, body, sent)
-    loop(body + 1, bodies, sent)
-
-    @pl.when(doubled)
-    def _():
-        twin_send().wait_send()
-
-    slip_swap.wait_send()
 
 
 def finish(updated, residual, updated_out, residual_out, sems):
@@ -464,7 +481,7 @@
         out_specs=(vmem, vmem),
         scratch_shapes=[
             pltpu.VMEM((rows, narrow), f32),
-            pltpu.VMEM(inverse.shape[1:], f32),
+            pltpu.VMEM((2, narrow, narrow), f32),
             pltpu.VMEM((3, count, blobs), f32),
             pltpu.VMEM((2, wide, wide), bf16),
             pltpu.VMEM((2, wide, wide), bf16),
@@ -482,7 +499,7 @@
             pltpu.VMEM((2, rows, wide), f32),
             pltpu.VMEM((2, wide, wide), bf16),
             pltpu.VMEM((2 * wide, 3 * wide), bf16),
-            dma((3,)),
+            dma((4,)),
             dma((2,)),
             dma((2,)),
             dma((bodies,)),

time: 11.3 us -> 11.2 us (level)
  Pallas kernels: 10.6 us -> 10.4 us
    pallas_call x1, Pallas kernels: 9.93 us -> 9.77 us  [local(): pl.pallas_call(functools.partial(kernel, row_count, col_count, blobs, ext...]
where the time goes in v4:
time: 11.2 us; the launch traced here: 11 us
  Pallas kernels  10.4 us (93%)
  between operations  0.64 us (6%)
    pallas_call x1, Pallas kernels, local(): pl.pallas_call(functools.partial(kernel, row_count, col_count, blobs, ext...  9.77 us
    pallas_call x1, Pallas kernels, local(): pl.pallas_call(finish, out_shape=(jax.ShapeDtypeStruct(slip.shape, f32),)...  0.63 us

profile of v4, /device:TPU:0, one launch (start us, length us, event | category | flops | bytes accessed | tf_op | source)
XLA Modules:
  0.0 11.0 jit_solution(13866139045434389456)
XLA Ops:
  0.6 9.8 %shard_map.50 = (f32[1,16,243]{2,1,0:T(8,128)S(1)}, f32[1,16,243]{2,1,0:T(8,128)S(1)}) custom-call(f32[1,16,243]{2,1,0:T(8,128)} %slip_hbm.1, f32[486,1,243]{2,1,0:T(1,128)} %bitcast.2, f32[3,16,81]{2,1,0:T(8,128)} %bitcast.3), custom_call_target="tpu_custom_call" | custom-call | tf_op jit(solution)/shard_map/pallas_call | solution.py:474
  10.4 0.6 %shard_map.51 = (f32[1,16,243]{2,1,0:T(8,128)}, f32[1,16,243]{2,1,0:T(8,128)}) custom-call(f32[1,16,243]{2,1,0:T(8,128)S(1)} %get-tuple-element.4.updated, f32[1,16,243]{2,1,0:T(8,128)S(1)} %get-tuple-element.5.residual), custom_call_target="tpu_custom_call" | custom-call | tf_op jit(solution)/shard_map/pallas_call | solution.py:517

commit v5 on v4

--- a/solution.py
+++ b/solution.py
@@ -30,8 +30,7 @@
     slip, inverse, positions,
     inv_high, inv_low, tiles, own_rows, own, source, other_slip, part, other_part,
     forces, twin_forces, held, base, far_part, turned, last,
-    load_sems, slip_sems, part_sems, send_sems, recv_sems, twin_sems,
-    go, ready,
+    load_sems, swap_sems, send_sems, recv_sems, go, ready,
 ):
     bodies = row_count * col_count // 2
     row = lax.axis_index("row")
@@ -42,7 +41,8 @@
     narrow = 3 * blobs
     wide = inv_high.shape[-1]
     pad = own.shape[2]
-    low_side = body < bodies // 2
+    middle = bodies // 2
+    low_side = body < middle
     lead = body == 0
 
     def far(step):
@@ -68,17 +68,29 @@
 
     barrier = pltpu.get_barrier_semaphore()
 
-    def swap(source_ref, target_ref, sems):
+    def greet(j):
+        there = 2 * j + jnp.where(lead, 0, 1)
+        signal(barrier, {"row": there // col_count, "col": lax.rem(there, col_count)})
+
+    def others(action):
+        loop(1, body, action)
+        loop(body + 1, bodies, action)
+
+    @pl.when(lead)
+    def _():
+        loop(1, bodies, greet)
+
+    def swap(source_ref, target_ref, which):
         return pltpu.make_async_remote_copy(
             src_ref=source_ref,
             dst_ref=target_ref,
-            send_sem=sems.at[0],
-            recv_sem=sems.at[1],
+            send_sem=swap_sems.at[0],
+            recv_sem=swap_sems.at[which],
             device_id={"col": partner},
             device_id_type=MESH,
         )
 
-    slip_swap = swap(slip_hbm.at[0], other_slip, slip_sems)
+    slip_swap = swap(slip_hbm.at[0], other_slip, 1)
 
     @pl.when(half == 1)
     def _():
@@ -103,25 +115,19 @@
     for load in (loads[0], *fetches, loads[1]):
         load.start()
 
-    def greet(j):
-        there = 2 * j + jnp.where(lead, 0, 1)
-        signal(barrier, {"row": there // col_count, "col": lax.rem(there, col_count)})
-
-    def others(action):
-        loop(1, body, action)
-        loop(body + 1, bodies, action)
-
-    others(greet)
+    @pl.when(jnp.logical_not(lead))
+    def _():
+        others(greet)
 
     @pl.when(half == 1)
     def _():
         loads[0].wait()
         pl.semaphore_wait(go.at[0], 1)
-        swap(slip, other_slip, slip_sems).start()
+        swap(slip, other_slip, 1).start()
 
     @pl.when(jnp.logical_not(lead))
     def _():
-        signal(ready.at[body], cross(0))
+        signal(ready.at[0], cross(0))
 
     inv_high[...] = jnp.zeros_like(inv_high)
     inv_low[...] = jnp.zeros_like(inv_low)
@@ -205,25 +211,28 @@
     forces[body] = force.astype(jnp.bfloat16)
     held[...] = force
 
+    slot = bodies - 1 - body
+
     def send(j):
+        to_lead = jnp.where(slot == 0, 2, jnp.where(slot < extra, 1, 0))
+        across = jnp.where(low_side == (j < middle), 0, 1)
         return pltpu.make_async_remote_copy(
             src_ref=forces.at[body],
             dst_ref=forces.at[body],
-            send_sem=send_sems.at[j],
-            recv_sem=recv_sems.at[body],
+            send_sem=send_sems.at[0],
+            recv_sem=recv_sems.at[jnp.where(j == 0, to_lead, across)],
             device_id=cross(j),
             device_id_type=MESH,
         )
 
-    slot = bodies - 1 - body
     doubled = (slot < extra) & jnp.logical_not(lead)
 
     def twin_send():
         return pltpu.make_async_remote_copy(
             src_ref=forces.at[body],
             dst_ref=twin_forces.at[slot],
-            send_sem=twin_sems.at[extra],
-            recv_sem=twin_sems.at[slot],
+            send_sem=send_sems.at[0],
+            recv_sem=recv_sems.at[jnp.where(slot == 0, 2, 1)],
             device_id=same(0),
             device_id_type=MESH,
         )
@@ -241,11 +250,11 @@
         @pl.when(jnp.logical_not(lead) & (half == 1))
         def _():
             pl.semaphore_wait(barrier, 2 * (bodies - 2))
-            signal(go.at[1], {"col": partner})
+            signal(go.at[0], {"col": partner})
 
         @pl.when(jnp.logical_not(lead) & (half == 0))
         def _():
-            pl.semaphore_wait(go.at[1], 1)
+            pl.semaphore_wait(go.at[0], 1)
 
     @pl.when(jnp.logical_not(lead))
     def _():
@@ -263,21 +272,13 @@
                 own_cols[:pad, 3 * t + a : 3 * t + a + 1], (pad, LANES)
             )
 
-    def send_on(j):
-        pl.semaphore_wait(ready.at[j], 1)
-        send(j).start()
-
     total_slots = jnp.where(lead, bodies + extra, bodies)
-    early = jnp.where(lead, bodies // 2 - 1, 0)
-    mid = jnp.where(lead, bodies // 2 + 1, 0)
-    lax.fori_loop(0, mid, build, 0)
-    loop(1, early + 1, send_on)
-    lax.fori_loop(mid, total_slots, build, 0)
+    lax.fori_loop(0, total_slots, build, 0)
 
     @pl.when(lead)
     def _():
-        loop(bodies // 2, bodies, send_on)
-
+        pl.semaphore_wait(ready.at[0], bodies - 1)
+        loop(1, bodies, lambda j: send(bodies - j).start())
 
     def product(values, j):
         return lax.dot_general(
@@ -287,48 +288,40 @@
             preferred_element_type=jnp.float32,
         )
 
-    def receive(j):
+    def several(count):
+        return pltpu.make_async_remote_copy(
+            src_ref=forces.at[pl.ds(0, count)],
+            dst_ref=forces.at[pl.ds(0, count)],
+            send_sem=send_sems.at[0],
+            recv_sem=recv_sems.at[0],
+            device_id={"col": partner},
+            device_id_type=MESH,
+        )
+
+    def receive(which, count):
         pltpu.make_async_remote_copy(
-            src_ref=forces.at[j],
-            dst_ref=forces.at[j],
+            src_ref=forces.at[pl.ds(0, count)],
+            dst_ref=forces.at[pl.ds(0, count)],
             send_sem=send_sems.at[0],
-            recv_sem=recv_sems.at[j],
+            recv_sem=recv_sems.at[which],
             device_id={"col": partner},
             device_id_type=MESH,
         ).wait_recv()
 
-    def twin_receive(f):
-        pltpu.make_async_remote_copy(
-            src_ref=twin_forces.at[f],
-            dst_ref=twin_forces.at[f],
-            send_sem=twin_sems.at[extra],
-            recv_sem=twin_sems.at[f],
-            device_id={"col": partner},
-            device_id_type=MESH,
-        ).wait_recv()
-
-    def gather(picks):
-        for j in picks:
-
-            @pl.when(j != body)
-            def _(j=j):
-                receive(j)
-
-        total = product(forces[picks[0]], picks[0])
-        for j in picks[1:]:
-            total = total + product(forces[j], j)
-        return total
-
-    def gather_run(start, stop):
-        if stop - start <= 8:
-            size = (stop - start + 1) // 2
-            total = gather([far(bodies - 1 - k) for k in range(start, start + size)])
-            return total + gather([far(bodies - 1 - k) for k in range(start + size, stop)])
+    def gather(start, stop):
+        picks = [far(bodies - 1 - k) for k in range(start, stop)] if stop - start <= 8 else None
+        if picks:
+            total = product(forces[picks[0]], picks[0])
+            for j in picks[1:]:
+                total = total + product(forces[j], j)
+            return total
+
+        def more(k, total):
+            j = far(bodies - 1 - k)
+            return total + product(forces[j], j)
+
         return lax.fori_loop(
-            start,
-            stop,
-            lambda k, total: total + gather([far(bodies - 1 - k)]),
-            jnp.zeros((slip.shape[0], 6 * pad), jnp.float32),
+            start, stop, more, jnp.zeros((slip.shape[0], 6 * pad), jnp.float32)
         )
 
     def compact(total):
@@ -351,24 +344,21 @@
             values.append(value[:, :wide])
         return values
 
-    def sent(j):
-        send(j).wait_send()
-
     def all_sent():
-        loop(0, body, sent)
-        loop(body + 1, bodies, sent)
-
         @pl.when(doubled)
         def _():
-            twin_send().wait_send()
-
-        slip_swap.wait_send()
-
-    part_swap = swap(part, other_part, part_sems)
+            several(bodies).wait_send()
+
+        @pl.when(jnp.logical_not(doubled))
+        def _():
+            several(bodies - 1).wait_send()
+
+    part_swap = swap(part, other_part, 2)
 
     def share(total):
         for t, value in enumerate(compact(total)):
             part[t] = value
+        slip_swap.wait_send()
         part_swap.start()
 
     def settle(more):
@@ -383,7 +373,10 @@
 
     @pl.when(jnp.logical_not(lead))
     def _():
-        share(gather_run(0, bodies))
+        receive(0, middle - 1)
+        total = gather(0, middle)
+        receive(1, middle)
+        share(total + gather(middle, bodies))
         mine, result = settle(False)
         residual[0] = mine
         updated[0] = result[:, :narrow]
@@ -408,17 +401,14 @@
                 turned[t] = tight
                 for side in (inv_high, inv_low):
                     folded = folded + jnp.dot(tight, side[t], preferred_element_type=jnp.float32)
-            high, low = split(folded)
             last[rows, :wide] = turned[half]
-            last[rows, wide : 2 * wide] = high
-            last[rows, 2 * wide :] = low
-
-        share(gather_run(0, bodies - extra))
+            last[rows, wide:] = folded.astype(jnp.bfloat16)
+
+        receive(0, bodies - extra - 1)
+        share(gather(0, bodies - extra))
 
         if extra > 1:
-            for f in range(1, extra):
-                receive(bodies - 1 - f)
-                twin_receive(f)
+            receive(1, 2 * (extra - 1))
             total = jnp.zeros((slip.shape[0], 6 * pad), jnp.float32)
             for f in range(1, extra):
                 total = total + product(forces[bodies - 1 - f], bodies - 1 - f)
@@ -430,16 +420,14 @@
         base[...] = mine
         held[...] = result
 
-        receive(bodies - 1)
-        twin_receive(0)
+        receive(2, 2)
         final = jnp.dot(
             jnp.concatenate([forces[bodies - 1], twin_forces[0]], axis=1),
             last[...],
             preferred_element_type=jnp.float32,
         )
         residual[0] = base[...] - final[:, :narrow]
-        change = final[:, wide : 2 * wide] + final[:, 2 * wide :]
-        updated[0] = (held[...] - change)[:, :narrow]
+        updated[0] = (held[...] - final[:, wide:])[:, :narrow]
 
 
 def finish(updated, residual, updated_out, residual_out, sems):
@@ -498,15 +486,13 @@
             pltpu.VMEM((rows, narrow), f32),
             pltpu.VMEM((2, rows, wide), f32),
             pltpu.VMEM((2, wide, wide), bf16),
-            pltpu.VMEM((2 * wide, 3 * wide), bf16),
+            pltpu.VMEM((2 * wide, 2 * wide), bf16),
             dma((4,)),
-            dma((2,)),
-            dma((2,)),
-            dma((bodies,)),
-            dma((bodies,)),
-            dma((extra + 1,)),
-            pltpu.SemaphoreType.REGULAR((2,)),
-            pltpu.SemaphoreType.REGULAR((bodies,)),
+            dma((3,)),
+            dma((1,)),
+            dma((3,)),
+            pltpu.SemaphoreType.REGULAR((1,)),
+            pltpu.SemaphoreType.REGULAR((1,)),
         ],
         compiler_params=pltpu.CompilerParams(
             collective_id=0,

time: 11.2 us -> 11 us (0.982)
  the two profiles are of different devices: /device:TPU:0 before, /device:TPU:13 now
where the time goes in v5:
time: 11 us; the launch traced here: 10.9 us
  Pallas kernels  10.3 us (94%)
  between operations  0.64 us (6%)
    pallas_call x1, Pallas kernels, local(): pl.pallas_call(functools.partial(kernel, row_count, col_count, blobs, ext...  9.62 us
    pallas_call x1, Pallas kernels, local(): pl.pallas_call(finish, out_shape=(jax.ShapeDtypeStruct(slip.shape, f32),)...  0.63 us

profile of v5, /device:TPU:13, one launch (start us, length us, event | category | flops | bytes accessed | tf_op | source)
XLA Modules:
  0.0 10.9 jit_solution(18298274020658176863)
XLA Ops:
  0.6 9.6 %shard_map.50 = (f32[1,16,243]{2,1,0:T(8,128)S(1)}, f32[1,16,243]{2,1,0:T(8,128)S(1)}) custom-call(f32[1,16,243]{2,1,0:T(8,128)} %slip_hbm.1, f32[486,1,243]{2,1,0:T(1,128)} %bitcast.2, f32[3,16,81]{2,1,0:T(8,128)} %bitcast.3), custom_call_target="tpu_custom_call" | custom-call | tf_op jit(solution)/shard_map/pallas_call | solution.py:462
  10.3 0.6 %shard_map.51 = (f32[1,16,243]{2,1,0:T(8,128)}, f32[1,16,243]{2,1,0:T(8,128)}) custom-call(f32[1,16,243]{2,1,0:T(8,128)S(1)} %get-tuple-element.4.updated, f32[1,16,243]{2,1,0:T(8,128)S(1)} %get-tuple-element.5.residual), custom_call_target="tpu_custom_call" | custom-call | tf_op jit(solution)/shard_map/pallas_call | solution.py:503

commit v6 on v5

--- a/solution.py
+++ b/solution.py
@@ -127,7 +127,7 @@
 
     @pl.when(jnp.logical_not(lead))
     def _():
-        signal(ready.at[0], cross(0))
+        signal(ready.at[jnp.where(low_side, 0, 1)], cross(0))
 
     inv_high[...] = jnp.zeros_like(inv_high)
     inv_low[...] = jnp.zeros_like(inv_low)
@@ -204,10 +204,11 @@
     def _():
         loads[0].wait()
 
+    force = apply(slip[...], half)
     fetches[1].wait()
     prepare(1 - half)
     slip_swap.wait_recv()
-    force = apply(slip[...], half) + apply(other_slip[...], 1 - half)
+    force = force + apply(other_slip[...], 1 - half)
     forces[body] = force.astype(jnp.bfloat16)
     held[...] = force
 
@@ -273,12 +274,20 @@
             )
 
     total_slots = jnp.where(lead, bodies + extra, bodies)
-    lax.fori_loop(0, total_slots, build, 0)
+    early_slots = jnp.where(lead, middle + 1, 0)
+    lax.fori_loop(0, early_slots, build, 0)
 
     @pl.when(lead)
     def _():
-        pl.semaphore_wait(ready.at[0], bodies - 1)
-        loop(1, bodies, lambda j: send(bodies - j).start())
+        pl.semaphore_wait(ready.at[0], middle - 1)
+        loop(1, middle, lambda j: send(j).start())
+
+    lax.fori_loop(early_slots, total_slots, build, 0)
+
+    @pl.when(lead)
+    def _():
+        pl.semaphore_wait(ready.at[1], bodies - middle)
+        loop(middle, bodies, lambda j: send(j).start())
 
     def product(values, j):
         return lax.dot_general(
@@ -492,7 +501,7 @@
             dma((1,)),
             dma((3,)),
             pltpu.SemaphoreType.REGULAR((1,)),
-            pltpu.SemaphoreType.REGULAR((1,)),
+            pltpu.SemaphoreType.REGULAR((2,)),
         ],
         compiler_params=pltpu.CompilerParams(
             collective_id=0,

time: 11 us -> 10.9 us (level)
  the two profiles are of different devices: /device:TPU:13 before, /device:TPU:0 now
where the time goes in v6:
time: 10.9 us; the launch traced here: 10.8 us
  Pallas kernels  10.1 us (93%)
  between operations  0.64 us (6%)
    pallas_call x1, Pallas kernels, local(): pl.pallas_call(functools.partial(kernel, row_count, col_count, blobs, ext...  9.52 us
    pallas_call x1, Pallas kernels, local(): pl.pallas_call(finish, out_shape=(jax.ShapeDtypeStruct(slip.shape, f32),)...  0.63 us

profile of v6, /device:TPU:0, one launch (start us, length us, event | category | flops | bytes accessed | tf_op | source)
XLA Modules:
  0.0 10.8 jit_solution(17421691410788512277)
XLA Ops:
  0.6 9.5 %shard_map.50 = (f32[1,16,243]{2,1,0:T(8,128)S(1)}, f32[1,16,243]{2,1,0:T(8,128)S(1)}) custom-call(f32[1,16,243]{2,1,0:T(8,128)} %slip_hbm.1, f32[486,1,243]{2,1,0:T(1,128)} %bitcast.2, f32[3,16,81]{2,1,0:T(8,128)} %bitcast.3), custom_call_target="tpu_custom_call" | custom-call | tf_op jit(solution)/shard_map/pallas_call | solution.py:471
  10.2 0.6 %shard_map.51 = (f32[1,16,243]{2,1,0:T(8,128)}, f32[1,16,243]{2,1,0:T(8,128)}) custom-call(f32[1,16,243]{2,1,0:T(8,128)S(1)} %get-tuple-element.4.updated, f32[1,16,243]{2,1,0:T(8,128)S(1)} %get-tuple-element.5.residual), custom_call_target="tpu_custom_call" | custom-call | tf_op jit(solution)/shard_map/pallas_call | solution.py:512

commit v7 on v6

--- a/solution.py
+++ b/solution.py
@@ -10,7 +10,7 @@
 MESH = pl.DeviceIdType.MESH
 LANES = 128
 CHUNK = 16
-EXTRA = 3
+EXTRA = 4
 
 
 def round_up(value, step):
@@ -108,11 +108,11 @@
     ]
     fetches = [
         pltpu.make_async_copy(
-            inverse_hbm.at[pl.ds(h * narrow, narrow), 0, :], inverse.at[h], load_sems.at[2 + k]
+            inverse_hbm.at[pl.ds(h * narrow, narrow), 0, :], inverse.at[h], load_sems.at[1 + k]
         )
         for k, h in enumerate((half, 1 - half))
     ]
-    for load in (loads[0], *fetches, loads[1]):
+    for load in (loads[0], *fetches):
         load.start()
 
     @pl.when(jnp.logical_not(lead))
@@ -198,6 +198,7 @@
         inv_low[h, :narrow, :narrow] = low
 
     fetches[0].wait()
+    loads[1].start()
     prepare(half)
 
     @pl.when(half == 0)
@@ -496,7 +497,7 @@
             pltpu.VMEM((2, rows, wide), f32),
             pltpu.VMEM((2, wide, wide), bf16),
             pltpu.VMEM((2 * wide, 2 * wide), bf16),
-            dma((4,)),
+            dma((3,)),
             dma((3,)),
             dma((1,)),
             dma((3,)),

time: 10.9 us -> 10.9 us (level)
  no operation moved by 1% of the time
where the time goes in v7:
time: 10.9 us; the launch traced here: 10.7 us
  Pallas kernels  10.1 us (93%)
  between operations  0.64 us (6%)
    pallas_call x1, Pallas kernels, local(): pl.pallas_call(functools.partial(kernel, row_count, col_count, blobs, ext...  9.47 us
    pallas_call x1, Pallas kernels, local(): pl.pallas_call(finish, out_shape=(jax.ShapeDtypeStruct(slip.shape, f32),)...  0.63 us

profile of v7, /device:TPU:0, one launch (start us, length us, event | category | flops | bytes accessed | tf_op | source)
XLA Modules:
  0.0 10.7 jit_solution(6074755063708910882)
XLA Ops:
  0.6 9.5 %shard_map.50 = (f32[1,16,243]{2,1,0:T(8,128)S(1)}, f32[1,16,243]{2,1,0:T(8,128)S(1)}) custom-call(f32[1,16,243]{2,1,0:T(8,128)} %slip_hbm.1, f32[486,1,243]{2,1,0:T(1,128)} %bitcast.2, f32[3,16,81]{2,1,0:T(8,128)} %bitcast.3), custom_call_target="tpu_custom_call" | custom-call | tf_op jit(solution)/shard_map/pallas_call | solution.py:472
  10.1 0.6 %shard_map.51 = (f32[1,16,243]{2,1,0:T(8,128)}, f32[1,16,243]{2,1,0:T(8,128)}) custom-call(f32[1,16,243]{2,1,0:T(8,128)S(1)} %get-tuple-element.4.updated, f32[1,16,243]{2,1,0:T(8,128)S(1)} %get-tuple-element.5.residual), custom_call_target="tpu_custom_call" | custom-call | tf_op jit(solution)/shard_map/pallas_call | solution.py:513

commit v8 on v7

--- a/solution.py
+++ b/solution.py
@@ -115,7 +115,7 @@
     for load in (loads[0], *fetches):
         load.start()
 
-    @pl.when(jnp.logical_not(lead))
+    @pl.when(jnp.logical_not(lead) & (half == 0))
     def _():
         others(greet)
 
@@ -251,7 +251,7 @@
 
         @pl.when(jnp.logical_not(lead) & (half == 1))
         def _():
-            pl.semaphore_wait(barrier, 2 * (bodies - 2))
+            pl.semaphore_wait(barrier, bodies - 2)
             signal(go.at[0], {"col": partner})
 
         @pl.when(jnp.logical_not(lead) & (half == 0))

time: 10.9 us -> 10.9 us (level)
  no operation moved by 1% of the time
where the time goes in v8:
time: 10.9 us; the launch traced here: 10.7 us
  Pallas kernels  10.1 us (93%)
  between operations  0.64 us (6%)
    pallas_call x1, Pallas kernels, local(): pl.pallas_call(functools.partial(kernel, row_count, col_count, blobs, ext...  9.46 us
    pallas_call x1, Pallas kernels, local(): pl.pallas_call(finish, out_shape=(jax.ShapeDtypeStruct(slip.shape, f32),)...  0.63 us

profile of v8, /device:TPU:0, one launch (start us, length us, event | category | flops | bytes accessed | tf_op | source)
XLA Modules:
  0.0 10.7 jit_solution(12387755175112393178)
XLA Ops:
  0.6 9.5 %shard_map.50 = (f32[1,16,243]{2,1,0:T(8,128)S(1)}, f32[1,16,243]{2,1,0:T(8,128)S(1)}) custom-call(f32[1,16,243]{2,1,0:T(8,128)} %slip_hbm.1, f32[486,1,243]{2,1,0:T(1,128)} %bitcast.2, f32[3,16,81]{2,1,0:T(8,128)} %bitcast.3), custom_call_target="tpu_custom_call" | custom-call | tf_op jit(solution)/shard_map/pallas_call | solution.py:472
  10.1 0.6 %shard_map.51 = (f32[1,16,243]{2,1,0:T(8,128)}, f32[1,16,243]{2,1,0:T(8,128)}) custom-call(f32[1,16,243]{2,1,0:T(8,128)S(1)} %get-tuple-element.4.updated, f32[1,16,243]{2,1,0:T(8,128)S(1)} %get-tuple-element.5.residual), custom_call_target="tpu_custom_call" | custom-call | tf_op jit(solution)/shard_map/pallas_call | solution.py:513
